TPU v7x, 32 devices: a whole 2x2x4 slice. The times are simulated.
32 devices in a mesh: ka: 16 (over z, y, core), aux: 2 (over x).
Axes of the slice: x: 2, y: 2, z: 4, core: 2. Of those that a mesh axis runs over, the one named last changes fastest.
Arguments:
- coefficients: bfloat16 [16, 4096, 128], P('ka'), may hold values from -2.09375 to 2.09375
- triple: bfloat16 [64, 2, 64, 768], P('aux'), may hold values from -0.5 to 0.5
- neighbors: int32 [64, 2], P('aux'), may hold values from 0 to 63
- w_screened: bfloat16 [16, 768, 1536], P('ka', 'aux'), as said below
- partner: int32 [2, 16], replicated, may hold values from 0 to 15, each once within a row
- q_ids: int32 [2], replicated, may hold values from 0 to 15
Outputs:
- sigma: float32 [16, 64, 128], P('ka', 'aux')
Inputs may be any that keep to these rules, and one draw needn't show every extreme that they name: Each stored w_screened is Hermitian: its real block is symmetric and its imaginary block antisymmetric.
All inputs are finite; a program needn't handle non-finite values.
Results may differ from a plain program's by a relative error of at most 0.0085.
Values may be sent and summed in bfloat16 or wider, within the bound.
A program may use at most 128 MiB of HBM per device.

v0:
```python
import functools
import math

import jax
import jax.numpy as jnp
from jax import lax
from jax.experimental import pallas as pl
from jax.experimental.pallas import tpu as pltpu
from jax.sharding import PartitionSpec as P

AUX_ATOM = 12
OCC = 16
GROUP = 4
JOINED = 4
VMEM = pltpu.VMEM
SMEM = pltpu.SMEM
DMA = pltpu.SemaphoreType.DMA
MESH = pl.DeviceIdType.MESH


def bit_of(me, b):
    return lax.rem(lax.div(me, 1 << b), 2)


def flipped(me, b):
    return me + (1 << b) - 2 * (1 << b) * bit_of(me, b)


def down_rows(n, rows):
    sizes = [rows]
    for _ in range(1, n.bit_length() - 1):
        rows = rows // 2 if rows // 2 % 16 == 0 else rows
        sizes.append(rows)
    return sizes


def remote(src, dst, send, recv, device):
    return pltpu.make_async_remote_copy(
        src_ref=src, dst_ref=dst, send_sem=send, recv_sem=recv, device_id=device, device_id_type=MESH
    )


def pick_bands(coef, src):
    rows = src.shape[1]
    orbitals, doubled = coef.shape
    high = 2 * OCC
    band = lax.broadcasted_iota(jnp.int32, (high, doubled), 0)
    col = lax.broadcasted_iota(jnp.int32, (high, doubled), 1)
    want = jnp.where(band < OCC, band, band - OCC + doubled // 2)
    choose = jnp.where(col == want, 1.0, 0.0).astype(jnp.bfloat16)
    step = 8
    for p0 in range(0, orbitals // 128, step):
        wide = lax.dot_general(
            choose,
            coef[p0 * 128 : (p0 + step) * 128, :],
            (((1,), (1,)), ((), ())),
            preferred_element_type=jnp.float32,
        ).astype(jnp.bfloat16)
        for p in range(p0, p0 + step):
            block = wide[:, (p - p0) * 128 : (p - p0 + 1) * 128]
            if rows >= high:
                at = p * high % rows
                src[p * high // rows, at : at + high, :] = block
            else:
                for i in range(high // rows):
                    src[p * (high // rows) + i] = block[i * rows : (i + 1) * rows]


def mask_weights(me, half, q_ref, w, kept, sent):
    size = w.shape[0]
    naux = w.shape[1] // 2
    own = pl.multiple_of(half * size, 128)
    other = pl.multiple_of((1 - half) * size, 128)
    first = me == q_ref[half]
    second = me == q_ref[1 - half]
    low = bit_of(me, 0) == 0
    tile = 64
    for r in range(0, size, tile):
        span = slice(r, r + tile)
        row = lax.broadcasted_iota(jnp.int32, (tile, size), 0) + r
        col = lax.broadcasted_iota(jnp.int32, (tile, size), 1)
        packed = jnp.where(
            row <= col,
            w[span, pl.ds(own, size)].astype(jnp.float32),
            w[span, pl.ds(own + naux, size)].astype(jnp.float32),
        ).astype(jnp.bfloat16)
        zero = jnp.zeros_like(packed)
        pieces = [
            jnp.where(first, packed, zero),
            jnp.where(first, w[span, pl.ds(other, size)], zero),
            jnp.where(second, packed, zero),
            jnp.where(first, w[span, pl.ds(other + naux, size)], zero),
        ]
        for i in range(2):
            at = slice(i * size + r, i * size + r + tile)
            kept[at] = jnp.where(low, pieces[i], pieces[2 + i])
            sent[at] = jnp.where(low, pieces[2 + i], pieces[i])


def place_far(t, transfers, landed, far):
    rows = landed.shape[2]
    high = 2 * OCC
    for p in range(far.shape[1]):
        if rows >= high:
            at = p * high % rows
            block = landed[t, p * high // rows, at : at + high, :]
        else:
            block = jnp.concatenate(
                [landed[t, p * (high // rows) + i] for i in range(high // rows)], axis=0
            )
        turned = pltpu.roll(block.astype(jnp.float32), 64, 1).astype(jnp.bfloat16)
        for r in range(2):
            at = (r * transfers + t) * OCC
            far[0, p, at : at + OCC, :] = block[r * OCC : (r + 1) * OCC]
            far[1, p, at : at + OCC, :] = turned[r * OCC : (r + 1) * OCC]


def pair_group(i, first_atom, nb_ref, far, triple, coef, own, part, stage):
    low = lax.broadcasted_iota(jnp.int32, (4 * OCC, 128), 1) < 64
    sign = jnp.where(lax.broadcasted_iota(jnp.int32, (64, 128), 1) < 64, 1.0, -1.0)
    zero = jnp.zeros((64, 128), jnp.bfloat16)
    for g in range(GROUP):
        c = i * GROUP + g
        n0 = nb_ref[0, c]
        n1 = nb_ref[1, c]
        x0 = far[lax.rem(n0, 2), lax.div(n0, 2)]
        x1 = far[1 - lax.rem(n1, 2), lax.div(n1, 2)]
        lhs = jnp.where(low, x0, x1)
        half = jnp.dot(lhs, triple[c], preferred_element_type=jnp.float32)
        half = half.astype(jnp.bfloat16)
        top, bottom = half[: 2 * OCC], half[2 * OCC :]
        at = pl.multiple_of((first_atom + c) * 64, 64)
        home = coef[pl.ds(at, 64), :].astype(jnp.float32)
        with_real = (home * sign).astype(jnp.bfloat16)
        with_imag = pltpu.roll(home, 64, 1).astype(jnp.bfloat16)
        rhs = jnp.concatenate(
            [
                jnp.concatenate([with_real, zero], axis=1),
                jnp.concatenate([zero, with_real], axis=1),
                jnp.concatenate([with_imag, zero], axis=1),
                jnp.concatenate([zero, with_imag], axis=1),
            ],
            axis=0,
        )
        rows = jnp.concatenate(
            [
                jnp.concatenate(
                    [top[:, s * 128 : (s + 1) * 128], bottom[:, s * 128 : (s + 1) * 128]], axis=1
                )
                for s in range(AUX_ATOM // 2)
            ],
            axis=0,
        )
        prod = jnp.dot(rows, rhs, preferred_element_type=jnp.float32)
        for s in range(AUX_ATOM // 2):
            for t in range(2):
                for b in range(2):
                    at = (g * AUX_ATOM + 2 * s + b) * OCC
                    r = s * 2 * OCC + t * OCC
                    stage[t, at : at + OCC, :] = prod[r : r + OCC, b * 128 : (b + 1) * 128]
    count = GROUP * AUX_ATOM
    for t, out in enumerate((own, part)):
        for l in range(OCC):
            out[i, l] = stage[t, pl.ds(l, count, stride=OCC), :].astype(jnp.bfloat16)


def unpack_weights(full, first, second, cross):
    size = first.shape[1]
    row = lax.broadcasted_iota(jnp.int32, (size, size), 0)
    col = lax.broadcasted_iota(jnp.int32, (size, size), 1)
    for piece, out in ((0, first), (2, second)):
        packed = full[piece * size : (piece + 1) * size].astype(jnp.float32)
        turned = packed.T
        out[:size] = jnp.where(row <= col, packed, turned).astype(jnp.bfloat16)
        signed = jnp.where(row > col, packed, -turned)
        out[size:] = jnp.where(row == col, 0.0, signed).astype(jnp.bfloat16)
    for i, piece in enumerate((1, 3)):
        block = full[piece * size : (piece + 1) * size].astype(jnp.float32)
        cross[i * size : (i + 1) * size] = block.T.astype(jnp.bfloat16)


def screen_bands(e, own, part, first, second, cross, zbuf, total):
    blocks, _, count, doubled = own.shape
    size = blocks * count
    sign = jnp.where(lax.broadcasted_iota(jnp.int32, (size, doubled), 1) < doubled // 2, -1.0, 1.0)

    def columns(x):
        return [
            jnp.concatenate([x[c, e * JOINED + i] for c in range(blocks)], axis=0)
            for i in range(JOINED)
        ]

    def apply(weights, wide, conj):
        prod = jnp.dot(weights[...], wide, preferred_element_type=jnp.float32)
        result = []
        for i in range(JOINED):
            re = prod[:size, i * doubled : (i + 1) * doubled]
            im = sign * pltpu.roll(prod[size:, i * doubled : (i + 1) * doubled], doubled // 2, 1)
            result.append((re - im if conj else re + im).astype(jnp.bfloat16))
        return result

    mine = columns(own)
    wide = jnp.concatenate(mine, axis=1)
    lefts = list(mine)
    screened = apply(first, wide, False)
    for i, z in enumerate(apply(cross, wide, True)):
        for c in range(blocks):
            zbuf[c, e * JOINED + i] = z[c * count : (c + 1) * count]
    theirs = columns(part)
    lefts += theirs
    screened += apply(second, jnp.concatenate(theirs, axis=1), False)
    total[...] += lax.dot_general(
        jnp.concatenate(lefts, axis=0),
        jnp.concatenate(screened, axis=0),
        (((0,), (0,)), ((), ())),
        preferred_element_type=jnp.float32,
    )


def sigma_kernel(
    n, prefactor, partner_ref, q_ref, nb_ref, coef_in, triple_in, w_in, out_ref,
    coef, triple, w, src, spread, picked, landed, far,
    kept, sent, accs, recvs, full, first, second, cross,
    own, part, incoming, zbuf, stage, total, give, got,
    local_sem, triple_sem, s1, r1, s2, r2, sw, rw, su, ru, sc, rc, sf, rf,
):
    me = lax.axis_index("ka")
    half = lax.axis_index("aux")
    transfers = partner_ref.shape[0]
    atoms = triple.shape[0]
    blocks = own.shape[0]
    bits = n.bit_length() - 1
    barrier = pltpu.get_barrier_semaphore()

    def greet(off, carry):
        dst = lax.rem(me + off, n)
        pl.semaphore_signal(barrier, inc=1, device_id={"ka": dst}, device_id_type=MESH)
        return carry

    lax.fori_loop(1, n, greet, 0)
    pl.semaphore_signal(barrier, inc=1, device_id={"aux": 1 - half}, device_id_type=MESH)

    get_coef = pltpu.make_async_copy(coef_in, coef, local_sem.at[0])
    get_w = pltpu.make_async_copy(w_in, w, local_sem.at[1])
    get_coef.start()
    get_w.start()

    def get_triple(i):
        span = pl.ds(i * GROUP, GROUP)
        return pltpu.make_async_copy(triple_in.at[span], triple.at[span], triple_sem.at[i])

    for i in range(blocks):
        get_triple(i).start()
    get_coef.wait()
    pick_bands(coef, src)
    pl.semaphore_wait(barrier, n)

    def over_peers(act):
        def body(off, carry):
            act(off, lax.rem(me + off, n))
            return carry

        lax.fori_loop(1, n, body, 0)

    def spread_copy(off, dst):
        return remote(src.at[dst], spread.at[me], s1.at[off], r1.at[off], {"ka": dst})

    def return_copy(t, off, dst):
        return remote(picked.at[t, dst], landed.at[t, me], s2.at[t, off], r2.at[t, off], {"ka": dst})

    over_peers(lambda off, dst: spread_copy(off, dst).start())
    spread[me] = src[me]

    sizes = down_rows(n, kept.shape[0])
    halved = [b == 0 or sizes[b] < sizes[b - 1] for b in range(bits)]
    starts, at = [], 0
    for b in range(bits):
        if halved[b]:
            at = at + bit_of(me, b) * sizes[b]
        starts.append(at)

    def down_copy(b):
        if b == 0:
            out = sent
        elif halved[b]:
            far_half = pl.multiple_of((1 - bit_of(me, b)) * sizes[b], 16)
            out = accs[b - 1].at[pl.ds(far_half, sizes[b])]
        else:
            out = accs[b - 1]
        return remote(out, recvs[b], sw.at[b], rw.at[b], {"ka": flipped(me, b)})

    def down_finish(b):
        down_copy(b).wait()
        if b == 0:
            mine = kept[...]
        elif halved[b]:
            near = pl.multiple_of(bit_of(me, b) * sizes[b], 16)
            mine = accs[b - 1][pl.ds(near, sizes[b])]
        else:
            mine = accs[b - 1][...]
        summed = mine + recvs[b][...]
        if b == bits - 1:
            full[pl.ds(pl.multiple_of(starts[b], 16), sizes[b])] = summed
        else:
            accs[b][...] = summed
            down_copy(b + 1).start()

    up_order = [b for b in reversed(range(bits)) if halved[b]]

    def up_copy(b):
        span = pl.ds(pl.multiple_of(starts[b], 16), sizes[b])
        return remote(full.at[span], full.at[span], su.at[b], ru.at[b], {"ka": flipped(me, b)})

    get_w.wait()
    mask_weights(me, half, q_ref, w, kept, sent)
    down_copy(0).start()
    down_finish(0)

    over_peers(lambda off, dst: spread_copy(off, dst).wait())
    for t in reversed(range(transfers)):
        which = lax.rem(half + t, transfers)

        def pick(k, carry, t=t, which=which):
            picked[t, k] = spread[partner_ref[which, k]]
            return carry

        lax.fori_loop(0, n, pick, 0)
        over_peers(lambda off, dst, t=t: return_copy(t, off, dst).start())
        landed[t, me] = picked[t, me]
    down_finish(1)
    for t in reversed(range(transfers)):
        over_peers(lambda off, dst, t=t: return_copy(t, off, dst).wait())
        place_far(t, transfers, landed, far)

    def cross_copy(i):
        return remote(part.at[i], incoming.at[i], sc.at[i], rc.at[i], {"aux": 1 - half})

    def pair(i, carry):
        get_triple(i).wait()
        pair_group(i, half * atoms, nb_ref, far, triple, coef, own, part, stage)
        cross_copy(i).start()
        return carry

    lax.fori_loop(0, blocks, pair, 0)
    for b in range(2, bits):
        down_finish(b)
    for b in up_order:
        up_copy(b).start()
        up_copy(b).wait()
    unpack_weights(full, first, second, cross)
    total[...] = jnp.zeros_like(total)

    def screen(e, carry):
        screen_bands(e, own, part, first, second, cross, zbuf, total)
        return carry

    lax.fori_loop(0, OCC // JOINED, screen, 0)
    total[...] = 0.5 * total[...]

    def meet(i, carry):
        cross_copy(i).wait()
        count = own.shape[2]
        total[...] += lax.dot_general(
            zbuf[i].reshape(OCC * count, 128),
            incoming[i].reshape(OCC * count, 128),
            (((0,), (0,)), ((), ())),
            preferred_element_type=jnp.float32,
        )
        return carry

    lax.fori_loop(0, blocks, meet, 0)
    value = total[...]
    bands = value.shape[0] // 2
    real = value[:bands, :bands] + value[bands:, bands:]
    imag = value[:bands, bands:] - value[bands:, :bands]
    sigma = prefactor * jnp.concatenate([real + real.T, imag - imag.T], axis=1)
    top, bottom = sigma[: bands // 2], sigma[bands // 2 :]
    low = half == 0
    give[...] = jnp.where(low, bottom, top)
    last = remote(give, got, sf.at[0], rf.at[0], {"aux": 1 - half})
    last.start()
    mine = jnp.where(low, top, bottom)
    last.wait()
    out_ref[...] = mine + got[...]


def local(n, coefficients, triple, neighbors, w_screened, partner, q_ids):
    transfers = partner.shape[0]
    coef = coefficients[0]
    orbitals, doubled = coef.shape
    atoms, neigh, per_atom, width = triple.shape
    size = w_screened.shape[1]
    naux = w_screened.shape[2] // 2
    prefactor = -1.0 / math.sqrt(transfers * naux * OCC)
    bits = n.bit_length() - 1
    blocks = atoms // GROUP
    pairs = orbitals // 128
    bf16 = jnp.bfloat16
    block = (n, pairs * 2 * OCC // n, 128)
    sizes = down_rows(n, 2 * size)
    chunk = (blocks, OCC, GROUP * AUX_ATOM, doubled)
    wide = (2 * size, size)
    scratch = [
        VMEM(coef.shape, bf16),
        VMEM((atoms, neigh * per_atom, width), bf16),
        VMEM(w_screened.shape[1:], bf16),
        VMEM(block, bf16),
        VMEM(block, bf16),
        VMEM((transfers,) + block, bf16),
        VMEM((transfers,) + block, bf16),
        VMEM((2, pairs, 2 * transfers * OCC, 128), bf16),
        VMEM(wide, bf16),
        VMEM(wide, bf16),
        [VMEM((rows, size), bf16) for rows in sizes[:-1]],
        [VMEM((rows, size), bf16) for rows in sizes],
        VMEM((4 * size, size), bf16),
        VMEM(wide, bf16),
        VMEM(wide, bf16),
        VMEM(wide, bf16),
        VMEM(chunk, bf16),
        VMEM(chunk, bf16),
        VMEM(chunk, bf16),
        VMEM(chunk, bf16),
        VMEM((2, GROUP * AUX_ATOM * OCC, 128), jnp.float32),
        VMEM((doubled, doubled), jnp.float32),
        VMEM((doubled // 4, doubled), jnp.float32),
        VMEM((doubled // 4, doubled), jnp.float32),
        DMA((2,)),
        DMA((blocks,)),
        DMA((n,)),
        DMA((n,)),
        DMA((transfers, n)),
        DMA((transfers, n)),
        DMA((bits,)),
        DMA((bits,)),
        DMA((bits,)),
        DMA((bits,)),
        DMA((blocks,)),
        DMA((blocks,)),
        DMA((1,)),
        DMA((1,)),
    ]
    any_spec = pl.BlockSpec(memory_space=pl.ANY)
    smem_spec = pl.BlockSpec(memory_space=SMEM)
    result = pl.pallas_call(
        functools.partial(sigma_kernel, n, prefactor),
        out_shape=jax.ShapeDtypeStruct((doubled // 4, doubled), jnp.float32),
        in_specs=[smem_spec] * 3 + [any_spec] * 3,
        out_specs=pl.BlockSpec(memory_space=VMEM),
        scratch_shapes=scratch,
        compiler_params=pltpu.CompilerParams(collective_id=0, has_side_effects=True),
        name="sigma",
    )(
        partner,
        q_ids,
        neighbors.T,
        coef,
        triple.reshape(atoms, neigh * per_atom, width),
        w_screened[0],
    )
    return result[None]


def solution(mesh):
    in_specs = (
        P("ka", None, None),
        P("aux", None, None, None),
        P("aux", None),
        P("ka", "aux", None),
        P(),
        P(),
    )
    return jax.shard_map(
        functools.partial(local, mesh.shape["ka"]),
        mesh=mesh,
        in_specs=in_specs,
        out_specs=P("ka", "aux", None),
        check_vma=False,
    )
```

profile of v0, /device:TPU:0, one launch (start us, length us, event | category | flops | bytes accessed | tf_op | source)
XLA Modules:
  0.0 71.1 jit_solution(7006444277979025924)
XLA Ops:
  0.0 69.8 %sigma.1 = f32[32,128]{1,0:T(8,128)} custom-call(s32[2,16]{1,0:T(2,128)} %partner_ref.1, s32[2]{0:T(128)} %q_ref.1, s32[2,32]{1,0:T(2,128)} %bitcast.9, bf16[4096,128]{1,0:T(8,128)(2,1)} %bitcast.7, bf16[32,128,768]{2,1,0:T(8,128)(2,1)} %bitcast.5, bf16[384,1536]{1,0:T(8,128)(2,1)} %bitcast.6), custom_call_target="tpu_custom_call" | custom-call | tf_op jit(solution)/shard_map/sigma/pallas_call | solution.py:445
  69.8 1.3 %copy.8 = f32[1,32,128]{2,1,0:T(8,128)} copy(f32[1,32,128]{2,1,0:T(8,128)} %bitcast.8) | data formatting | bytes 32768
where the time goes:
time: 71.4 us; the launch traced here: 71.1 us
  Pallas kernels  69.8 us (98%)
  local copies, waits for them, and re-layouts  1.32 us (2%)
    pallas_call x1, Pallas kernels, local(): pl.pallas_call(functools.partial(sigma_kernel, n, prefactor), out_shape=j...  69.8 us

commit v1 on v0

v1 whole, which is shorter than its diff:
```python
import functools
import math

import jax
import jax.numpy as jnp
from jax import lax
from jax.experimental import pallas as pl
from jax.experimental.pallas import tpu as pltpu
from jax.sharding import PartitionSpec as P

AUX_ATOM = 12
OCC = 16
GROUP = 4
JOINED = 4
SHARE = ((1, 2), (2, 1), (1, 2))
EARLY = 3
ORDER = (
    "first0", "first1", "spread", "back", "second0", "second1", "relay00", "far0", "middle1",
    "middle0", "far1", "relay20", "relay10", "swap0", "turn1", "swap1", "pair0", "pair1", "turn0",
    "relay11", "pair2", "pair3", "up1", "up0", "relay01", "pair4", "pair5", "pair6", "pair7",
    "rest1", "rest0", "relay21", "relay12", "relay02", "done1", "done0", "screen", "relay22",
    "names", "other0", "other1", "other2",
)
VMEM = pltpu.VMEM
SMEM = pltpu.SMEM
DMA = pltpu.SemaphoreType.DMA
MESH = pl.DeviceIdType.MESH


def bit_of(me, b):
    return lax.rem(lax.div(me, 1 << b), 2)


def flipped(me, b):
    return me + (1 << b) - 2 * (1 << b) * bit_of(me, b)


def down_rows(n, rows):
    sizes = []
    bits = n.bit_length() - 1
    for b in range(bits):
        rows = rows // 2 if rows // 2 % 16 == 0 and b < bits - 1 else rows
        sizes.append(rows)
    return sizes


class Lane:
    def __init__(self, me, order, sent, kept, full, accs, recvs, sems):
        self.me, self.order = me, order
        self.sent, self.kept, self.full, self.accs, self.recvs = sent, kept, full, accs, recvs
        self.sizes = [x.shape[0] for x in recvs]
        rows = full.shape[0]
        self.halved, self.starts, at = [], [], 0
        for b, size in zip(order, self.sizes):
            self.halved.append(size < rows)
            if size < rows:
                at = at + bit_of(me, b) * size
            self.starts.append(pl.multiple_of(at, 16))
            rows = size
        self.down_send, self.down_recv, self.up_send, self.up_recv = sems

    def peer(self, s):
        return {"ka": flipped(self.me, self.order[s])}

    def down(self, s):
        if s == 0:
            out = self.sent
        elif self.halved[s]:
            away = pl.multiple_of((1 - bit_of(self.me, self.order[s])) * self.sizes[s], 16)
            out = self.accs[s - 1].at[pl.ds(away, self.sizes[s])]
        else:
            out = self.accs[s - 1]
        return remote(out, self.recvs[s], self.down_send.at[s], self.down_recv.at[s], self.peer(s))

    def step(self, s):
        self.down(s).wait()
        if s == 0:
            mine = self.kept[...]
        elif self.halved[s]:
            near = pl.multiple_of(bit_of(self.me, self.order[s]) * self.sizes[s], 16)
            mine = self.accs[s - 1][pl.ds(near, self.sizes[s])]
        else:
            mine = self.accs[s - 1][...]
        summed = mine + self.recvs[s][...]
        if s == len(self.order) - 1:
            self.full[pl.ds(self.starts[s], self.sizes[s])] = summed
        else:
            self.accs[s][...] = summed
            self.down(s + 1).start()

    def up(self, s):
        span = pl.ds(self.starts[s], self.sizes[s])
        return remote(
            self.full.at[span], self.full.at[span], self.up_send.at[s], self.up_recv.at[s], self.peer(s)
        )


def remote(src, dst, send, recv, device):
    return pltpu.make_async_remote_copy(
        src_ref=src, dst_ref=dst, send_sem=send, recv_sem=recv, device_id=device, device_id_type=MESH
    )


def pick_bands(first, coef, src):
    rows = src.shape[1]
    doubled = coef.shape[1]
    high = 2 * OCC
    pairs = src.shape[0] * rows // high
    band = lax.broadcasted_iota(jnp.int32, (high, doubled), 0)
    col = lax.broadcasted_iota(jnp.int32, (high, doubled), 1)
    want = jnp.where(band < OCC, band, band - OCC + doubled // 2)
    choose = jnp.where(col == want, 1.0, 0.0).astype(jnp.bfloat16)
    step = min(8, pairs)
    for p0 in range(0, pairs, step):
        wide = lax.dot_general(
            choose,
            coef[pl.ds(pl.multiple_of(first + p0 * 128, 128), step * 128), :],
            (((1,), (1,)), ((), ())),
            preferred_element_type=jnp.float32,
        ).astype(jnp.bfloat16)
        for p in range(p0, p0 + step):
            block = wide[:, (p - p0) * 128 : (p - p0 + 1) * 128]
            if rows >= high:
                at = p * high % rows
                src[p * high // rows, at : at + high, :] = block
            else:
                for i in range(high // rows):
                    src[p * (high // rows) + i] = block[i * rows : (i + 1) * rows]


def mask_weights(me, half, q_ref, w, kept, sent):
    size = w.shape[0]
    naux = w.shape[1] // 2
    own = pl.multiple_of(half * size, 128)
    other = pl.multiple_of((1 - half) * size, 128)
    first = me == q_ref[half]
    second = me == q_ref[1 - half]
    low = bit_of(me, 0) == 0
    tile = 64
    for r in range(0, size, tile):
        span = slice(r, r + tile)
        row = lax.broadcasted_iota(jnp.int32, (tile, size), 0) + r
        col = lax.broadcasted_iota(jnp.int32, (tile, size), 1)
        packed = jnp.where(
            row <= col,
            w[span, pl.ds(own, size)].astype(jnp.float32),
            w[span, pl.ds(own + naux, size)].astype(jnp.float32),
        ).astype(jnp.bfloat16)
        zero = jnp.zeros_like(packed)
        pieces = [
            jnp.where(first, packed, zero),
            jnp.where(second, packed, zero),
            jnp.where(first, w[span, pl.ds(other, size)], zero),
            jnp.where(first, w[span, pl.ds(other + naux, size)], zero),
        ]
        for i in range(2):
            lower, upper = pieces[2 * i : 2 * i + 2]
            kept[i][span] = jnp.where(low, lower, upper)
            sent[i][span] = jnp.where(low, upper, lower)


def place_far(t, transfers, first, landed, far):
    rows = landed.shape[1]
    high = 2 * OCC
    for p in range(landed.shape[0] * rows // high):
        if rows >= high:
            at = p * high % rows
            block = landed[p * high // rows, at : at + high, :]
        else:
            block = jnp.concatenate(
                [landed[p * (high // rows) + i] for i in range(high // rows)], axis=0
            )
        turned = pltpu.roll(block.astype(jnp.float32), 64, 1).astype(jnp.bfloat16)
        for r in range(2):
            at = pl.multiple_of((r * transfers + t) * OCC, OCC)
            far[0, first + p, pl.ds(at, OCC), :] = block[r * OCC : (r + 1) * OCC]
            far[1, first + p, pl.ds(at, OCC), :] = turned[r * OCC : (r + 1) * OCC]


def pair_group(first_atom, nb_ref, far, triple, coef, outs, stage):
    low = lax.broadcasted_iota(jnp.int32, (4 * OCC, 128), 1) < 64
    sign = jnp.where(lax.broadcasted_iota(jnp.int32, (64, 128), 1) < 64, 1.0, -1.0)
    zero = jnp.zeros((64, 128), jnp.bfloat16)
    for g in range(GROUP):
        n0 = nb_ref(0, g)
        n1 = nb_ref(1, g)
        x0 = far[lax.rem(n0, 2), lax.div(n0, 2)]
        x1 = far[1 - lax.rem(n1, 2), lax.div(n1, 2)]
        lhs = jnp.where(low, x0, x1)
        half = jnp.dot(lhs, triple(g), preferred_element_type=jnp.float32)
        half = half.astype(jnp.bfloat16)
        top, bottom = half[: 2 * OCC], half[2 * OCC :]
        at = pl.multiple_of((first_atom + g) * 64, 64)
        home = coef[pl.ds(at, 64), :].astype(jnp.float32)
        with_real = (home * sign).astype(jnp.bfloat16)
        with_imag = pltpu.roll(home, 64, 1).astype(jnp.bfloat16)
        rhs = jnp.concatenate(
            [
                jnp.concatenate([with_real, zero], axis=1),
                jnp.concatenate([zero, with_real], axis=1),
                jnp.concatenate([with_imag, zero], axis=1),
                jnp.concatenate([zero, with_imag], axis=1),
            ],
            axis=0,
        )
        rows = jnp.concatenate(
            [
                jnp.concatenate(
                    [top[:, s * 128 : (s + 1) * 128], bottom[:, s * 128 : (s + 1) * 128]], axis=1
                )
                for s in range(AUX_ATOM // 2)
            ],
            axis=0,
        )
        prod = jnp.dot(rows, rhs, preferred_element_type=jnp.float32)
        for s in range(AUX_ATOM // 2):
            for t in outs:
                for b in range(2):
                    at = (g * AUX_ATOM + 2 * s + b) * OCC
                    r = s * 2 * OCC + t * OCC
                    stage[t, at : at + OCC, :] = prod[r : r + OCC, b * 128 : (b + 1) * 128]
    count = GROUP * AUX_ATOM
    for t, out in outs.items():
        for l in range(OCC):
            out[l] = stage[t, pl.ds(l, count, stride=OCC), :].astype(jnp.bfloat16)


def unpack_diagonal(packed, upper, lower):
    size = packed.shape[1]
    cut = upper.shape[0] // 2
    row = lax.broadcasted_iota(jnp.int32, (size, size), 0)
    col = lax.broadcasted_iota(jnp.int32, (size, size), 1)
    value = packed.astype(jnp.float32)
    turned = value.T
    real = jnp.where(row <= col, value, turned)
    imag = jnp.where(row > col, value, -turned)
    imag = jnp.where(row == col, 0.0, imag)
    twice = jnp.where(lax.broadcasted_iota(jnp.int32, (cut, size), 1) < cut, 1.0, 2.0)
    upper[:cut] = (twice * real[:cut]).astype(jnp.bfloat16)
    upper[cut:] = (twice * imag[:cut]).astype(jnp.bfloat16)
    lower[: size - cut] = real[cut:, cut:].astype(jnp.bfloat16)
    lower[size - cut :] = imag[cut:, cut:].astype(jnp.bfloat16)


def unpack_cross(full, cross):
    size = full.shape[1]
    for i in range(2):
        span = slice(i * size, (i + 1) * size)
        cross[span] = full[span].astype(jnp.float32).T.astype(jnp.bfloat16)


def columns(x, e):
    return [
        jnp.concatenate([x[c, e * JOINED + i] for c in range(x.shape[0])], axis=0)
        for i in range(JOINED)
    ]


def apply(weights, wide, conj):
    size = weights.shape[0] // 2
    sign = jnp.where(lax.broadcasted_iota(jnp.int32, (size, 128), 1) < 64, -1.0, 1.0)
    prod = jnp.dot(weights[...], wide, preferred_element_type=jnp.float32)
    result = []
    for i in range(JOINED):
        re = prod[:size, i * 128 : (i + 1) * 128]
        im = sign * pltpu.roll(prod[size:, i * 128 : (i + 1) * 128], 64, 1)
        result.append((re - im if conj else re + im).astype(jnp.bfloat16))
    return result


def gram(left, right):
    return lax.dot_general(left, right, (((0,), (0,)), ((), ())), preferred_element_type=jnp.float32)


def diagonal(parts, upper, lower):
    cut = upper.shape[0] // 2
    wide = jnp.concatenate(parts, axis=1)
    first = apply(upper, wide, False)
    rest = apply(lower, wide[cut:], False)
    return [part for both in zip(first, rest) for part in both]


def screen_bands(e, own, part, uppers, lowers, cross, zbuf, total):
    count = own.shape[2]
    mine = columns(own, e)
    for i, z in enumerate(apply(cross, jnp.concatenate(mine, axis=1), True)):
        for c in range(own.shape[0]):
            zbuf[c, e * JOINED + i] = z[c * count : (c + 1) * count]
    theirs = columns(part, e)
    screened = diagonal(mine, uppers[0], lowers[0]) + diagonal(theirs, uppers[1], lowers[1])
    total[...] += gram(jnp.concatenate(mine + theirs, axis=0), jnp.concatenate(screened, axis=0))


def sigma_kernel(
    n, prefactor, partner_ref, q_ref, nb_ref, nb_in, coef_in, triple_in, w_in, out_ref,
    coef, triple, w, src, spread, picked, landed, swapped, far,
    kept, sent, accs, recvs, full, uppers, lowers, cross,
    own, part, incoming, zbuf, stage, total, give, got, other, nb_land, nb_other,
    local_sem, triple_sem, s1, r1, s2, r2, s3, r3, lane_sems, sc, rc, sf, rf, fetch_sems,
):
    me = lax.axis_index("ka")
    half = lax.axis_index("aux")
    transfers = partner_ref.shape[0]
    atoms = triple.shape[0] // 2
    group_rows = 2 * GROUP
    blocks = own.shape[0]
    fetched = len(SHARE)
    crossing = blocks - fetched
    bits = n.bit_length() - 1
    across = {"aux": 1 - half}
    barrier = pltpu.get_barrier_semaphore()

    def greet(off, carry):
        dst = lax.rem(me + off, n)
        pl.semaphore_signal(barrier, inc=1, device_id={"ka": dst}, device_id_type=MESH)
        return carry

    lax.fori_loop(1, n, greet, 0)
    pl.semaphore_signal(barrier, inc=1, device_id=across, device_id_type=MESH)

    def get_coef(near):
        rows = coef.shape[0] // 2
        span = pl.ds(pl.multiple_of((half if near else 1 - half) * rows, 128), rows)
        return pltpu.make_async_copy(coef_in.at[span], coef.at[span], local_sem.at[0 if near else 2])

    get_w = pltpu.make_async_copy(w_in, w, local_sem.at[1])
    get_coef(True).start()
    get_w.start()

    def get_triple(i):
        span = pl.ds(i * group_rows, group_rows)
        return pltpu.make_async_copy(triple_in.at[span], triple.at[span], triple_sem.at[i])

    def over_peers(act):
        def body(off, carry):
            act(off, lax.rem(me + off, n))
            return carry

        lax.fori_loop(1, n, body, 0)

    def spread_copy(off, dst):
        return remote(src.at[dst], spread.at[me], s1.at[off], r1.at[off], {"ka": dst})

    def return_copy(t, off, dst):
        return remote(picked.at[t, dst], landed.at[t, me], s2.at[t, off], r2.at[t, off], {"ka": dst})

    core = bit_of(me, 0)
    nb_copy = remote(nb_in, nb_land, sf.at[1], rf.at[1], across)

    def swap(t):
        return remote(landed.at[t], swapped.at[t], s3.at[t], r3.at[t], across)

    def piece(i, level):
        bits_of = SHARE[i] + (0,)
        size = group_rows >> len(bits_of)
        at = 0
        for j in range(level, len(bits_of)):
            at = at + (size << j) * bit_of(me, bits_of[j])
        return at, size << level

    def fetch(i):
        at, size = piece(i, 0)
        return remote(
            triple_in.at[pl.ds((crossing + i) * group_rows + at, size)],
            other.at[i, pl.ds(at, size)],
            fetch_sems[0].at[i],
            fetch_sems[1].at[i],
            across,
        )

    def pass_on(i, level):
        at, size = piece(i, level)
        span = other.at[i, pl.ds(at, size)]
        peer = {"ka": flipped(me, (SHARE[i] + (0,))[level])}
        return remote(span, span, fetch_sems[2].at[i, level], fetch_sems[3].at[i, level], peer)

    def relay(i, level):
        if level == 0:
            fetch(i).wait()
        else:
            pass_on(i, level - 1).wait()
        pass_on(i, level).start()

    lanes = [
        Lane(me, order, sent[i], kept[i], full[i], accs[i], recvs[i], lane_sems[i])
        for i, order in enumerate(lane_orders(bits))
    ]

    tops = [s for s in reversed(range(bits)) if lanes[0].halved[s]]

    def raise_lane(lane, i):
        if i > 0:
            lane.up(tops[i - 1]).wait()
        if i < len(tops):
            lane.up(tops[i]).start()

    def cross_copy(i):
        return remote(part.at[i], incoming.at[i], sc.at[i], rc.at[i], across)

    def pair(i, outs):
        pair_group(
            half * atoms + i * GROUP,
            lambda j, g: nb_ref[j, i * GROUP + g],
            far,
            lambda g: triple[pl.ds((i * GROUP + g) * 2, 2)].reshape(128, triple.shape[2]),
            coef,
            outs,
            stage,
        )

    def pair_mine(i):
        get_triple(i).wait()
        pair(i, {0: own.at[i], 1: part.at[i]})
        if i < crossing:
            cross_copy(i).start()

    def pair_other(i):
        pass_on(i, len(SHARE[i])).wait()
        pair_group(
            (1 - half) * atoms + (crossing + i) * GROUP,
            lambda j, g: nb_other[j, (crossing + i) * GROUP + g],
            far,
            lambda g: other[i, 2 * g : 2 * g + 2].reshape(128, triple.shape[2]),
            coef,
            {0: incoming.at[crossing + i]},
            stage,
        )

    def send_back(t):
        over_peers(lambda off, dst: return_copy(t, off, dst).start())

    get_coef(True).wait()
    pick_bands(half * (coef.shape[0] // 2), coef, src)
    get_w.wait()
    mask_weights(me, half, q_ref, w, kept, sent)
    pl.semaphore_wait(barrier, n)
    over_peers(lambda off, dst: spread_copy(off, dst).start())
    for lane in lanes:
        lane.down(0).start()
    nb_copy.start()
    for i in range(EARLY):
        fetch(i).start()
    spread[me] = src[me]
    get_coef(False).start()
    for i in range(blocks):
        get_triple(i).start()

    def pick(t):
        def body(k, carry):
            picked[t, k] = spread[partner_ref[t, k]]
            return carry

        lax.fori_loop(0, n, body, 0)
        landed[t, me] = picked[t, me]

    def spread_done():
        over_peers(lambda off, dst: spread_copy(off, dst).wait())
        for t in range(transfers):
            pick(t)
            if t == 0:
                send_back(t)

    far_half = far.shape[1] // 2

    def returned(t):
        over_peers(lambda off, dst: return_copy(t, off, dst).wait())
        swap(t).start()
        place_far(lax.rem(half + t, 2), transfers, half * far_half, landed.at[t], far)

    def exchanged(t):
        swap(t).wait()
        place_far(lax.rem(half + t, 2), transfers, (1 - half) * far_half, swapped.at[t], far)

    def fetch_rest():
        for i in range(EARLY, fetched):
            fetch(i).start()

    def middle(lane):
        for s in range(2, bits - 1):
            lane.step(s)

    def last_down(lane):
        lane.step(bits - 1)
        raise_lane(lane, 0)

    def rest_up(lane):
        for i in range(2, len(tops)):
            raise_lane(lane, i)

    def names_done():
        get_coef(False).wait()
        nb_copy.wait()
        move = pltpu.make_async_copy(nb_land, nb_other, local_sem.at[3])
        move.start()
        move.wait()

    def lane_done(i):
        raise_lane(lanes[i], len(tops))
        if i == 0:
            size = cross.shape[1]
            for j in range(2):
                unpack_diagonal(full[0][j * size : (j + 1) * size], uppers[j], lowers[j])
        else:
            unpack_cross(full[1], cross)

    def loop(start, stop, body):
        lax.fori_loop(start, stop, body, 0)

    def screen(e, carry):
        screen_bands(e, own, part, uppers, lowers, cross, zbuf, total)
        return carry

    steps = {
        "spread": spread_done,
        "back": lambda: send_back(1),
        "fetch": fetch_rest,
        "names": names_done,
        "screen": lambda: loop(0, OCC // JOINED, screen),
    }
    for i in range(blocks):
        steps[f"pair{i}"] = functools.partial(pair_mine, i)
    for t in range(transfers):
        steps[f"far{t}"] = functools.partial(returned, t)
        steps[f"swap{t}"] = functools.partial(exchanged, t)
    for i, lane in enumerate(lanes):
        steps[f"first{i}"] = functools.partial(lane.step, 0)
        steps[f"second{i}"] = functools.partial(lane.step, 1)
        steps[f"middle{i}"] = functools.partial(middle, lane)
        steps[f"turn{i}"] = functools.partial(last_down, lane)
        steps[f"up{i}"] = functools.partial(raise_lane, lane, 1)
        steps[f"rest{i}"] = functools.partial(rest_up, lane)
        steps[f"done{i}"] = functools.partial(lane_done, i)
    for i in range(fetched):
        for level in range(len(SHARE[i]) + 1):
            steps[f"relay{i}{level}"] = functools.partial(relay, i, level)
        steps[f"other{i}"] = functools.partial(pair_other, i)
    total[...] = jnp.zeros_like(total)
    for name in ORDER:
        steps[name]()
    total[...] = 0.5 * total[...]

    def meet(i):
        count = own.shape[2]
        total[...] += gram(
            zbuf[i].reshape(OCC * count, 128), incoming[i].reshape(OCC * count, 128)
        )

    def meet_other(i, carry):
        meet(i)
        return carry

    def meet_sent(i, carry):
        cross_copy(i).wait()
        meet(i)
        return carry

    lax.fori_loop(crossing, blocks, meet_other, 0)
    lax.fori_loop(0, crossing, meet_sent, 0)
    value = total[...]
    bands = value.shape[0] // 2
    real = value[:bands, :bands] + value[bands:, bands:]
    imag = value[:bands, bands:] - value[bands:, :bands]
    sigma = prefactor * jnp.concatenate([real + real.T, imag - imag.T], axis=1)
    top, bottom = sigma[: bands // 2], sigma[bands // 2 :]
    low = half == 0
    give[...] = jnp.where(low, bottom, top)
    last = remote(give, got, sf.at[0], rf.at[0], across)
    last.start()
    mine = jnp.where(low, top, bottom)
    last.wait()
    out_ref[...] = mine + got[...]


def lane_orders(bits):
    order = list(range(bits))
    return [order, [0, 2, 1] + order[3:]]


def local(n, coefficients, triple, neighbors, w_screened, partner, q_ids):
    transfers = partner.shape[0]
    coef = coefficients[0]
    orbitals, doubled = coef.shape
    atoms, neigh, per_atom, width = triple.shape
    size = w_screened.shape[1]
    naux = w_screened.shape[2] // 2
    prefactor = -1.0 / math.sqrt(transfers * naux * OCC)
    bits = n.bit_length() - 1
    blocks = atoms // GROUP
    pairs = orbitals // 128
    bf16 = jnp.bfloat16
    block = (n, pairs * OCC // n, 128)
    sizes = down_rows(n, 2 * size)
    lanes = 2
    cut = size % 256
    fetched = len(SHARE)
    chunk = (blocks, OCC, GROUP * AUX_ATOM, doubled)
    wide = (2 * size, size)
    scratch = [
        VMEM(coef.shape, bf16),
        VMEM((atoms * neigh, per_atom, width), bf16),
        VMEM(w_screened.shape[1:], bf16),
        VMEM(block, bf16),
        VMEM(block, bf16),
        VMEM((transfers,) + block, bf16),
        VMEM((transfers,) + block, bf16),
        VMEM((transfers,) + block, bf16),
        VMEM((2, pairs, 2 * transfers * OCC, 128), bf16),
        [VMEM((size, size), bf16)] * lanes,
        [VMEM((size, size), bf16)] * lanes,
        [[VMEM((rows, size), bf16) for rows in sizes[:-1]]] * lanes,
        [[VMEM((rows, size), bf16) for rows in sizes]] * lanes,
        [VMEM(wide, bf16)] * lanes,
        [VMEM((2 * cut, size), bf16)] * lanes,
        [VMEM((2 * (size - cut), size - cut), bf16)] * lanes,
        VMEM(wide, bf16),
        VMEM(chunk, bf16),
        VMEM(chunk, bf16),
        VMEM(chunk, bf16),
        VMEM(chunk, bf16),
        VMEM((transfers, GROUP * AUX_ATOM * OCC, 128), jnp.float32),
        VMEM((doubled, doubled), jnp.float32),
        VMEM((doubled // 4, doubled), jnp.float32),
        VMEM((doubled // 4, doubled), jnp.float32),
        VMEM((fetched, GROUP * neigh, per_atom, width), bf16),
        VMEM((neigh, atoms), jnp.int32),
        SMEM((neigh, atoms), jnp.int32),
        DMA((4,)),
        DMA((blocks,)),
        DMA((n,)),
        DMA((n,)),
        DMA((transfers, n)),
        DMA((transfers, n)),
        DMA((transfers,)),
        DMA((transfers,)),
        [[DMA((bits,))] * 4] * lanes,
        DMA((blocks,)),
        DMA((blocks,)),
        DMA((2,)),
        DMA((2,)),
        [DMA((fetched,))] * 2 + [DMA((fetched, 3))] * 2,
    ]
    any_spec = pl.BlockSpec(memory_space=pl.ANY)
    smem_spec = pl.BlockSpec(memory_space=SMEM)
    result = pl.pallas_call(
        functools.partial(sigma_kernel, n, prefactor),
        out_shape=jax.ShapeDtypeStruct((doubled // 4, doubled), jnp.float32),
        in_specs=[smem_spec] * 3 + [any_spec] * 4,
        out_specs=pl.BlockSpec(memory_space=VMEM),
        scratch_shapes=scratch,
        compiler_params=pltpu.CompilerParams(collective_id=0, has_side_effects=True),
        name="sigma",
    )(
        partner,
        q_ids,
        neighbors.T,
        neighbors.T,
        coef,
        triple.reshape(atoms * neigh, per_atom, width),
        w_screened[0],
    )
    return result[None]


def solution(mesh):
    in_specs = (
        P("ka", None, None),
        P("aux", None, None, None),
        P("aux", None),
        P("ka", "aux", None),
        P(),
        P(),
    )
    return jax.shard_map(
        functools.partial(local, mesh.shape["ka"]),
        mesh=mesh,
        in_specs=in_specs,
        out_specs=P("ka", "aux", None),
        check_vma=False,
    )
```

time: 71.4 us -> 55 us (0.77)
  Pallas kernels: 69.8 us -> 53.4 us
    pallas_call x1, Pallas kernels: 69.8 us -> 53.4 us  [local(): pl.pallas_call(functools.partial(sigma_kernel, n, prefactor), out_shape=j...]
where the time goes in v1:
time: 55 us; the launch traced here: 54.7 us
  Pallas kernels  53.4 us (97%)
  local copies, waits for them, and re-layouts  1.32 us (2%)
    pallas_call x1, Pallas kernels, local(): pl.pallas_call(functools.partial(sigma_kernel, n, prefactor), out_shape=j...  53.4 us
    unnamed x1, local copies, waits for them, and re-layouts  1.32 us

profile of v1, /device:TPU:0, one launch (start us, length us, event | category | flops | bytes accessed | tf_op | source)
XLA Modules:
  0.0 54.7 jit_solution(13635534609954137194)
XLA Ops:
  0.0 53.4 %sigma.1 = f32[32,128]{1,0:T(8,128)} custom-call(s32[2,16]{1,0:T(2,128)} %partner_ref.1, s32[2]{0:T(128)} %q_ref.1, s32[2,32]{1,0:T(2,128)} %bitcast.9, s32[2,32]{1,0:T(2,128)} %bitcast.10, bf16[4096,128]{1,0:T(8,128)(2,1)} %bitcast.7, bf16[64,64,768]{2,1,0:T(8,128)(2,1)} %bitcast.5, bf16[384,1536]{1,0:T(8,128)(2,1)} %bitcast.6), custom_call_target="tpu_custom_call" | custom-call | tf_op jit(solution)/shard_map/sigma/pallas_call | solution.py:644
  53.4 1.3 %copy.8 = f32[1,32,128]{2,1,0:T(8,128)} copy(f32[1,32,128]{2,1,0:T(8,128)} %bitcast.8) | data formatting | bytes 32768

commit v2 on v1

--- a/solution.py
+++ b/solution.py
@@ -235,11 +235,11 @@
     real = jnp.where(row <= col, value, turned)
     imag = jnp.where(row > col, value, -turned)
     imag = jnp.where(row == col, 0.0, imag)
-    twice = jnp.where(lax.broadcasted_iota(jnp.int32, (cut, size), 1) < cut, 1.0, 2.0)
-    upper[:cut] = (twice * real[:cut]).astype(jnp.bfloat16)
-    upper[cut:] = (twice * imag[:cut]).astype(jnp.bfloat16)
-    lower[: size - cut] = real[cut:, cut:].astype(jnp.bfloat16)
-    lower[size - cut :] = imag[cut:, cut:].astype(jnp.bfloat16)
+    scale = jnp.where(lax.broadcasted_iota(jnp.int32, (cut, size), 1) < cut, 0.5, 1.0)
+    upper[:cut] = (scale * real[:cut]).astype(jnp.bfloat16)
+    upper[cut:] = (scale * imag[:cut]).astype(jnp.bfloat16)
+    lower[: size - cut] = (0.5 * real[cut:, cut:]).astype(jnp.bfloat16)
+    lower[size - cut :] = (0.5 * imag[cut:, cut:]).astype(jnp.bfloat16)
 
 
 def unpack_cross(full, cross):
@@ -537,7 +537,6 @@
     total[...] = jnp.zeros_like(total)
     for name in ORDER:
         steps[name]()
-    total[...] = 0.5 * total[...]
 
     def meet(i):
         count = own.shape[2]

time: 55 us -> 55 us (level)
  no operation moved by 1% of the time
where the time goes in v2:
time: 55 us; the launch traced here: 54.7 us
  Pallas kernels  53.4 us (97%)
  local copies, waits for them, and re-layouts  1.32 us (2%)
    pallas_call x1, Pallas kernels, local(): pl.pallas_call(functools.partial(sigma_kernel, n, prefactor), out_shape=j...  53.4 us
    unnamed x1, local copies, waits for them, and re-layouts  1.32 us

profile of v2, /device:TPU:0, one launch (start us, length us, event | category | flops | bytes accessed | tf_op | source)
XLA Modules:
  0.0 54.7 jit_solution(9614943424825041595)
XLA Ops:
  0.0 53.4 %sigma.1 = f32[32,128]{1,0:T(8,128)} custom-call(s32[2,16]{1,0:T(2,128)} %partner_ref.1, s32[2]{0:T(128)} %q_ref.1, s32[2,32]{1,0:T(2,128)} %bitcast.9, s32[2,32]{1,0:T(2,128)} %bitcast.10, bf16[4096,128]{1,0:T(8,128)(2,1)} %bitcast.7, bf16[64,64,768]{2,1,0:T(8,128)(2,1)} %bitcast.5, bf16[384,1536]{1,0:T(8,128)(2,1)} %bitcast.6), custom_call_target="tpu_custom_call" | custom-call | tf_op jit(solution)/shard_map/sigma/pallas_call | solution.py:643
  53.4 1.3 %copy.8 = f32[1,32,128]{2,1,0:T(8,128)} copy(f32[1,32,128]{2,1,0:T(8,128)} %bitcast.8) | data formatting | bytes 32768
